TPU v7x, 128 devices: a whole 4x4x4 slice. The times are simulated.
128 devices in a mesh: ws: 8 (over y_hi, z), seq: 16 (over x, y_lo, core).
Axes of the slice: x: 4, y: 4 (y_hi: 2, y_lo: 2; y = y_hi * 2 + y_lo), z: 4, core: 2. Of those that a mesh axis runs over, the one named last changes fastest.
Arguments:
- tokens: bfloat16 [8, 6144, 1536], P('ws', 'seq'), may hold values from -16 to 16
- w_same: bfloat16 [1536, 1536], replicated, may hold values from -0.15625 to 0.15625
- w_partner: bfloat16 [1536, 1536], replicated, may hold values from -0.15625 to 0.15625
- w_query: bfloat16 [1536, 1024], replicated, may hold values from -0.15625 to 0.15625
- w_key: bfloat16 [1536, 128], replicated, may hold values from -0.15625 to 0.15625
- w_value: bfloat16 [1536, 192], replicated, may hold values from -0.15625 to 0.15625
- w_out: bfloat16 [1536, 1536], replicated, may hold values from -0.15625 to 0.15625
Outputs:
- attended: bfloat16 [8, 6144, 1536], P('ws', 'seq')
All inputs are finite; a program needn't handle non-finite values.
Results may differ from a plain program's by a relative error of at most 0.012.
Values may be sent and summed in bfloat16 or wider, within the bound.
A program may use at most 192 MiB of HBM per device.

v0:
```python
import jax
import jax.numpy as jnp
from jax import lax
from jax.sharding import PartitionSpec as P


def swapped(value, axis, bit):
    mask = 2**bit
    pairs = [(source, source ^ mask) for source in range(lax.axis_size(axis))]
    return lax.ppermute(value, axis, pairs)


def body(tokens, w_same, w_partner, w_query, w_key, w_value, w_out):
    count = lax.axis_size("seq")
    local = tokens[0]
    partner = swapped(tokens, "ws", 0)
    for level in range(count.bit_length() - 1):
        partner = swapped(partner, "seq", level)
    mirrored = jnp.flip(partner[0], 0)
    hidden = (
        jnp.dot(local, w_same, preferred_element_type=jnp.float32)
        + jnp.dot(mirrored, w_partner, preferred_element_type=jnp.float32)
    ).astype(jnp.bfloat16)
    query = jnp.dot(hidden, w_query, preferred_element_type=jnp.float32).astype(jnp.bfloat16)
    keys = jnp.dot(hidden, w_key, preferred_element_type=jnp.float32).astype(jnp.bfloat16)
    values = jnp.dot(hidden, w_value, preferred_element_type=jnp.float32).astype(jnp.bfloat16)
    rows = local.shape[0]
    key_width = w_key.shape[1]
    value_width = w_value.shape[1]
    head_count = w_query.shape[1] // key_width
    query_rows = query.reshape(rows * head_count, key_width)
    factor = key_width ** (-0.5)
    top = jnp.full((rows * head_count,), -jnp.inf, jnp.float32)
    total = jnp.zeros((rows * head_count,), jnp.float32)
    accum = jnp.zeros((rows * head_count, value_width), jnp.float32)
    scores = (
        lax.dot_general(
            query_rows,
            lax.all_gather(keys, "seq", axis=0, tiled=True),
            (((1,), (1,)), ((), ())),
            preferred_element_type=jnp.float32,
        )
        * factor
    )
    peak = jnp.max(scores, axis=1)
    decay = jnp.exp(top - peak)
    weights = jnp.exp(scores - peak[:, None])
    total = total * decay + jnp.sum(weights, axis=1)
    accum = accum * decay[:, None] + jnp.dot(
        weights.astype(jnp.bfloat16),
        lax.all_gather(values, "seq", axis=0, tiled=True),
        preferred_element_type=jnp.float32,
    )
    peak, total, accum = (peak, total, accum)
    mixed = (accum / total[:, None]).astype(jnp.bfloat16).reshape(rows, head_count * value_width)
    result = jnp.dot(mixed, w_out, preferred_element_type=jnp.float32).astype(jnp.bfloat16)
    return result[None]


def solution(mesh):
    placed = (P("ws", "seq", None), P(), P(), P(), P(), P(), P())
    return jax.shard_map(
        body, mesh=mesh, in_specs=placed, out_specs=P("ws", "seq", None), check_vma=False
    )
```

profile of v0, /device:TPU:1, one launch (start us, length us, event | category | flops | bytes accessed | tf_op | source)
XLA Modules:
  0.0 282.5 jit_solution(16489391349393364194)
XLA Ops:
  6.5 0.0 copy-start
  6.5 0.0 all-gather.3.cloned.1.call-start
  6.5 2.5 collective-permute-start
  9.0 25.9 %collective-permute-done = bf16[1,384,1536]{2,1,0:T(8,128)(2,1)S(1)} collective-permute-done((bf16[1,384,1536]{2,1,0:T(8,128)(2,1)}, bf16[1,384,1536]{2,1,0:T(8,128)(2,1)S(1)}, u32[]{:S(2)}, u32[]{:S(2)}) %collective-permute-start) | collective-permute-done | bytes 1179680 | tf_op jit(solution)/shard_map/ppermute | solution.py:10
  34.9 1.3 collective-permute-start.1
  36.1 2.5 collective-permute-done.1
  38.6 1.3 collective-permute-start.2
  39.9 25.9 %collective-permute-done.2 = bf16[1,384,1536]{2,1,0:T(8,128)(2,1)S(1)} collective-permute-done((bf16[1,384,1536]{2,1,0:T(8,128)(2,1)S(1)}, bf16[1,384,1536]{2,1,0:T(8,128)(2,1)S(1)}, u32[]{:S(2)}, u32[]{:S(2)}) %collective-permute-start.2) | collective-permute-done | bytes 1179680 | tf_op jit(solution)/shard_map/ppermute | solution.py:10
  65.8 1.2 collective-permute-start.3
  67.0 25.1 %collective-permute-done.3 = bf16[1,384,1536]{2,1,0:T(8,128)(2,1)S(1)} collective-permute-done((bf16[1,384,1536]{2,1,0:T(8,128)(2,1)S(1)}, bf16[1,384,1536]{2,1,0:T(8,128)(2,1)S(1)}, u32[]{:S(2)}, u32[]{:S(2)}) %collective-permute-start.3) | collective-permute-done | bytes 1179680 | tf_op jit(solution)/shard_map/ppermute | solution.py:10
  92.1 2.7 collective-permute-start.4
  94.8 6.1 %fusion.15 = f32[384,1536]{1,0:T(8,128)} fusion(bf16[1536,1536]{1,0:T(8,128)(2,1)} %param.8, bf16[1,384,1536]{2,1,0:T(8,128)(2,1)} %param.7), kind=kOutput, calls=%fused_computation.13 | convolution fusion | flops 1811939328 | bytes 8257536 | tf_op jit(solution)/shard_map/dot_general | solution.py:21
  100.9 18.2 %collective-permute-done.4 = bf16[1,384,1536]{2,1,0:T(8,128)(2,1)} collective-permute-done((bf16[1,384,1536]{2,1,0:T(8,128)(2,1)S(1)}, bf16[1,384,1536]{2,1,0:T(8,128)(2,1)}, u32[]{:S(2)}, u32[]{:S(2)}) %collective-permute-start.4) | collective-permute-done | bytes 1179680 | tf_op jit(solution)/shard_map/ppermute | solution.py:10
  119.1 17.4 %rev.4 = bf16[384,1536]{1,0:T(8,128)(2,1)} reverse(bf16[384,1536]{1,0:T(8,128)(2,1)} %bitcast.1), dimensions={0} | reverse | bytes 2359296 | tf_op jit(solution)/shard_map/jit(_flip)/rev | solution.py:19
  136.5 0.0 copy-start.2
  136.6 5.5 %fusion.13 = bf16[384,1536]{1,0:T(8,128)(2,1)S(1)} fusion(f32[384,1536]{1,0:T(8,128)} %fusion.15, bf16[384,1536]{1,0:T(8,128)(2,1)} %rev.4, bf16[1536,1536]{1,0:T(8,128)(2,1)} %param.9), kind=kOutput, calls=%fused_computation.10 | convolution fusion | flops 1813118976 | bytes 9437184 | tf_op jit(solution)/shard_map/dot_general | solution.py:22
  142.0 0.0 copy-start.1
  142.0 1.0 copy-done.1
  143.0 0.0 copy-done.2
  143.0 1.1 convolution_convert_fusion.3
  144.2 0.0 all-gather.3.cloned.1.call-update
  144.2 0.2 all-gather.5.cloned.1.call-start
  144.4 0.0 copy-done
  144.4 3.5 %convolution_convert_fusion.1 = bf16[384,1024]{1,0:T(8,128)(2,1)} fusion(bf16[384,1536]{1,0:T(8,128)(2,1)} %copy-done.1, bf16[1536,1024]{1,0:T(8,128)(2,1)S(1)} %copy-done), kind=kOutput, calls=%fused_computation.12 | convolution fusion | flops 1208352768 | bytes 5111808 | tf_op jit(solution)/shard_map/dot_general | solution.py:24
  148.0 2.2 reshape.17
  150.2 2.6 convolution_convert_fusion.2
  152.8 0.0 all-gather.5.cloned.1.call-update
  152.8 29.2 %all-gather.3.cloned.1.call-done = bf16[6144,128]{1,0:T(8,128)(2,1)} async-done(((bf16[384,128]{1,0:T(8,128)(2,1)}), bf16[6144,128]{1,0:T(8,128)(2,1)}) %all-gather.3.cloned.1.call-update) | async-done | bytes 1572880 | tf_op jit(solution)/shard_map/all_gather | solution.py:39
  182.0 29.3 %multiply_reduce_fusion = (f32[3072]{0:T(1024)S(1)}, f32[3072,6144]{1,0:T(8,128)}) fusion(bf16[3072,128]{1,0:T(8,128)(2,1)} %reshape.17, bf16[6144,128]{1,0:T(8,128)(2,1)} %all-gather.3.cloned.1.call-done), kind=kOutput, calls=%fused_computation.1 | convolution fusion | flops 4869583872 | bytes 77869056 | tf_op jit(solution)/shard_map/dot_general | solution.py:37
  211.3 23.8 %fusion = f32[3072]{0:T(1024)S(1)} fusion(f32[3072,6144]{1,0:T(8,128)} %get-tuple-element.8, f32[3072]{0:T(1024)S(1)} %get-tuple-element.7), kind=kLoop, calls=%fused_computation.2 | loop fusion | flops 56620032 | bytes 75522048 | tf_op jit(solution)/shard_map/reduce_sum | solution.py:48
  235.1 0.0 all-gather.5.cloned.1.call-done
  235.2 28.5 %fusion.10 = bf16[3072,192]{0,1:T(8,128)(2,1)} fusion(bf16[6144,192]{1,0:T(8,128)(2,1)} %all-gather.5.cloned.1.call-done, f32[3072,6144]{1,0:T(8,128)} %get-tuple-element.8, f32[3072]{0:T(1024)S(1)} %get-tuple-element.7, f32[3072]{0:T(1024)S(1)} %get-tuple-element.6, f32[3072]{0:T(1024)S(1)} %get-tuple-element.5), kind=kOutput, calls=%fused_computation.7 | convolution fusion | flops 7306149888 | bytes 79073280 | tf_op jit(solution)/shard_map/dot_general | solution.py:49
  263.6 2.5 copy.8
  266.2 3.8 %reshape.18 = bf16[384,1536]{1,0:T(8,128)(2,1)} reshape(bf16[3072,192]{1,0:T(8,128)(2,1)} %copy.8) | data formatting | bytes 2359296 | tf_op jit(solution)/shard_map/reshape | solution.py:55
  269.9 5.7 %fusion.14 = bf16[1,384,1536]{2,1,0:T(8,128)(2,1)} fusion(bf16[384,1536]{1,0:T(8,128)(2,1)} %reshape.18, bf16[1536,1536]{1,0:T(8,128)(2,1)} %param.13), kind=kOutput, calls=%fused_computation.11 | convolution fusion | flops 1812529152 | bytes 7077888 | tf_op jit(solution)/shard_map/dot_general | solution.py:56
  (1 shorter events, 0.0 us)
Async XLA Ops:
  6.5 137.9 %copy-start = (bf16[1536,1024]{1,0:T(8,128)(2,1)S(1)}, bf16[1536,1024]{1,0:T(8,128)(2,1)}, u32[]{:S(2)}) copy-start(bf16[1536,1024]{1,0:T(8,128)(2,1)} %param.10) | copy-start | bytes 9437188
  6.5 175.5 %all-gather.3.cloned.1.call-start = ((), (), s32[]{:S(2)}) async-start(), calls=%async_computation | async-start | bytes 1671168 | tf_op jit(solution)/shard_map/all_gather | solution.py:39
  6.5 28.3 %collective-permute-start = (bf16[1,384,1536]{2,1,0:T(8,128)(2,1)}, bf16[1,384,1536]{2,1,0:T(8,128)(2,1)S(1)}, u32[]{:S(2)}, u32[]{:S(2)}) collective-permute-start(bf16[1,384,1536]{2,1,0:T(8,128)(2,1)} %param.7), channel_id=1, source_target_pairs={{0,16},{16,0},{32,48},{48,32},{64,80},{80,64},{96,112},{112,96},{1... | collective-permute-start | bytes 3538952 | tf_op jit(solution)/shard_map/ppermute | solution.py:10
  34.9 3.7 %collective-permute-start.1 = (bf16[1,384,1536]{2,1,0:T(8,128)(2,1)S(1)}, bf16[1,384,1536]{2,1,0:T(8,128)(2,1)S(1)}, u32[]{:S(2)}, u32[]{:S(2)}) collective-permute-start(bf16[1,384,1536]{2,1,0:T(8,128)(2,1)S(1)} %collective-permute-done), channel_id=1, source_target_pairs={{0,1},{1,0},{2,3},{3,2},{4,5},{5,4},{6,7},{7,6},{8,9},{9,8},{10,11... | collective-permute-start | bytes 3538952 | tf_op jit(solution)/shard_map/ppermute | solution.py:10
  38.6 27.2 %collective-permute-start.2 = (bf16[1,384,1536]{2,1,0:T(8,128)(2,1)S(1)}, bf16[1,384,1536]{2,1,0:T(8,128)(2,1)S(1)}, u32[]{:S(2)}, u32[]{:S(2)}) collective-permute-start(bf16[1,384,1536]{2,1,0:T(8,128)(2,1)S(1)} %collective-permute-done.1), channel_id=1, source_target_pairs={{0,2},{1,3},{2,0},{3,1},{4,6},{5,7},{6,4},{7,5},{8,10},{9,11},{10,... | collective-permute-start | bytes 3538952 | tf_op jit(solution)/shard_map/ppermute | solution.py:10
  65.8 26.3 %collective-permute-start.3 = (bf16[1,384,1536]{2,1,0:T(8,128)(2,1)S(1)}, bf16[1,384,1536]{2,1,0:T(8,128)(2,1)S(1)}, u32[]{:S(2)}, u32[]{:S(2)}) collective-permute-start(bf16[1,384,1536]{2,1,0:T(8,128)(2,1)S(1)} %collective-permute-done.2), channel_id=1, source_target_pairs={{0,4},{1,5},{2,6},{3,7},{4,0},{5,1},{6,2},{7,3},{8,12},{9,13},{10,... | collective-permute-start | bytes 3538952 | tf_op jit(solution)/shard_map/ppermute | solution.py:10
  92.1 27.1 %collective-permute-start.4 = (bf16[1,384,1536]{2,1,0:T(8,128)(2,1)S(1)}, bf16[1,384,1536]{2,1,0:T(8,128)(2,1)}, u32[]{:S(2)}, u32[]{:S(2)}) collective-permute-start(bf16[1,384,1536]{2,1,0:T(8,128)(2,1)S(1)} %collective-permute-done.3), channel_id=1, source_target_pairs={{0,8},{1,9},{2,10},{3,11},{4,12},{5,13},{6,14},{7,15},{8,0},{9,1},... | collective-permute-start | bytes 3538952 | tf_op jit(solution)/shard_map/ppermute | solution.py:10
  136.5 6.5 %copy-start.2 = (bf16[1536,128]{1,0:T(8,128)(2,1)S(1)}, bf16[1536,128]{1,0:T(8,128)(2,1)}, u32[]{:S(2)}) copy-start(bf16[1536,128]{1,0:T(8,128)(2,1)} %param.11) | copy-start | bytes 1179652
  142.0 1.0 copy-start.1
  144.2 91.0 %all-gather.5.cloned.1.call-start = ((), (), s32[]{:S(2)}) async-start(), calls=%async_computation.1 | async-start | bytes 3342336 | tf_op jit(solution)/shard_map/all_gather | solution.py:51
Sparse Core Ops, SparseCore 0:
  144.3 37.6 all-gather.2
  183.7 35.3 all-gather.4
where the time goes:
time: 285 us; the launch traced here: 282 us
  waiting for transfers between devices  127 us (45%)
  matrix products  82.3 us (29%)
  local copies, waits for them, and re-layouts  27 us (9%)
  other arithmetic  23.8 us (8%)
  between operations  13.5 us (5%)
  starting transfers between devices  9.18 us (3%)
    ppermute x5, waiting for transfers between devices, swapped(): return lax.ppermute(value, axis, pairs)  97.5 us
    dot_general x1, matrix products, body(): lax.dot_general(query_rows, lax.all_gather(keys, 'seq', axis=0, tiled=Tru...  29.3 us
    all_gather x1, waiting for transfers between devices, body(): lax.all_gather(keys, 'seq', axis=0, tiled=True)  29.2 us
    dot_general x1, matrix products, body(): jnp.dot(weights.astype(jnp.bfloat16), lax.all_gather(values, 'seq', axis=...  28.5 us
    reduce_sum x1, other arithmetic, body(): total = total * decay + jnp.sum(weights, axis=1)  23.8 us
    rev x1, local copies, waits for them, and re-layouts, body(): mirrored = jnp.flip(partner[0], 0)  17.4 us
    ppermute x5, starting transfers between devices, swapped(): return lax.ppermute(value, axis, pairs)  8.96 us
    dot_general x1, matrix products, body(): jnp.dot(local, w_same, preferred_element_type=jnp.float32)  6.1 us
  transfers between devices with their start and end apart: 7, of which 6 were waited for; matrix products, arithmetic and copies ran while one was open for 24% of the time, Pallas kernels for 0%

commit v1 on v0

v1 whole, which is shorter than its diff:
```python
import functools
import math

import jax
import jax.numpy as jnp
from jax import lax
from jax.experimental import pallas as pl
from jax.experimental.pallas import tpu as pltpu
from jax.sharding import PartitionSpec as P

MESH = pl.DeviceIdType.MESH
F32 = jnp.float32
BF16 = jnp.bfloat16
NT = (((1,), (1,)), ((), ()))

Y, H, M = 1, 2, 4
ORDER = (0, H, Y, M, Y ^ H, M ^ H, Y ^ M, Y ^ M ^ H)
PLACE = {slot: place for place, slot in enumerate(ORDER)}
SENDS = ((0, Y), (0, M), (0, H), (Y, H), (M, H), (M, Y), (Y ^ M, H))


def kernel(
    dims,
    tok, w_same, w_partner, w_query, w_key, w_value_t, w_out,
    out_ref,
    tok_v, flip_v, same_v, partner_v, query_v, key_v, value_v, out_v, hid_v,
    kv_out, kv_in, kv_mine, kv_all, keys_v, vals_v,
    qb_out, qb_in, qa_v, q_v, peak_v, acc_v, sum_v,
    load_sem, pair_send, pair_recv, ring_send, ring_recv, core_send, core_recv,
):
    rows, width, heads, dk, dv = dims
    chunks = heads // 2
    half = rows // 2
    ws = lax.axis_index("ws")
    seq = lax.axis_index("seq")
    last = lax.axis_size("seq") - 1
    x, y, core = seq // 4, (seq // 2) % 2, seq % 2
    pair = {"ws": ws + 1 - 2 * (ws % 2), "seq": last - seq}
    other = {"ws": ws, "seq": seq + 1 - 2 * core}
    link = {
        Y: {"ws": ws, "seq": seq + 2 - 4 * y},
        H: {"ws": ws, "seq": seq + 4 - 8 * (x % 2)},
        M: {"ws": ws, "seq": (3 - x) * 4 + y * 2 + core},
    }

    loads = [pltpu.make_async_copy(tok.at[0], tok_v, load_sem.at[0])]
    tiles = width // 256
    for n in range(tiles):
        loads.append(pltpu.make_async_copy(w_partner.at[:, pl.ds(n * 256, 256)], partner_v.at[n], load_sem.at[1 + n]))
    base = 1 + tiles
    rest = (
        (w_key, key_v),
        (w_value_t, value_v.at[pl.ds(0, dv)]),
        (w_value_t.at[pl.ds(128, dv - 128)], value_v.at[pl.ds(dv, dv - 128)]),
    )
    for n, (src, dst) in enumerate(rest):
        loads.append(pltpu.make_async_copy(src, dst, load_sem.at[base + n]))
    q_base = base + len(rest)
    for n in range(chunks):
        loads.append(pltpu.make_async_copy(w_query.at[:, pl.ds(n * 256, 256)], query_v.at[n], load_sem.at[q_base + n]))
    s_base = q_base + chunks
    for n in range(tiles):
        loads.append(pltpu.make_async_copy(w_same.at[:, pl.ds(n * 256, 256)], same_v.at[n], load_sem.at[s_base + n]))
    o_base = s_base + tiles
    loads.append(pltpu.make_async_copy(w_out, out_v, load_sem.at[o_base]))
    for copy in loads:
        copy.start()

    barrier = pltpu.get_barrier_semaphore()
    for peer in (pair, other, link[Y], link[H], link[M]):
        pl.semaphore_signal(barrier, inc=1, device_id=peer, device_id_type=MESH)

    loads[0].wait()
    turned = lax.broadcasted_iota(jnp.int32, (rows, rows), 0) + lax.broadcasted_iota(jnp.int32, (rows, rows), 1)
    turn = jnp.where(turned == rows - 1, 1.0, 0.0).astype(BF16)
    for n in range(tiles):
        flip_v[:, n * 256:(n + 1) * 256] = jnp.dot(
            turn, tok_v[:, n * 256:(n + 1) * 256], preferred_element_type=F32
        ).astype(BF16)
    for n in range(tiles):
        loads[1 + n].wait()
        hid_v[:, n * 256:(n + 1) * 256] = jnp.dot(flip_v[...], partner_v[n], preferred_element_type=F32).astype(BF16)

    def key_value():
        hidden = hid_v[...]
        k = jnp.dot(hidden, key_v[...], preferred_element_type=F32)
        v = lax.dot_general(hidden, value_v[...], NT, preferred_element_type=F32)
        lane = lax.broadcasted_iota(jnp.int32, (half, 128), 1)
        tail = jnp.where(lane < dv - 128, v[:half, 128:], v[half:, 128:])
        return k, v[:, :128], tail

    for n in range(len(rest)):
        loads[base + n].wait()
    k, v, tail = key_value()
    kv_out[0:rows] = k.astype(BF16)
    kv_out[rows:2 * rows] = v.astype(BF16)
    kv_out[2 * rows:] = tail.astype(BF16)

    def query_out(n):
        loads[q_base + n].wait()
        q = jnp.dot(hid_v[...], query_v[n], preferred_element_type=F32).astype(BF16)
        qb_out[n, 0:rows] = q[:, :128]
        qb_out[n, rows:] = q[:, 128:]

    query_out(0)
    pl.semaphore_wait(barrier, 5)
    kv_copy = pltpu.make_async_remote_copy(
        src_ref=kv_out, dst_ref=kv_in, send_sem=pair_send.at[0], recv_sem=pair_recv.at[0],
        device_id=pair, device_id_type=MESH,
    )
    kv_copy.start()
    q_copies = [
        pltpu.make_async_remote_copy(
            src_ref=qb_out.at[n], dst_ref=qb_in.at[n], send_sem=pair_send.at[1 + n], recv_sem=pair_recv.at[1 + n],
            device_id=pair, device_id_type=MESH,
        )
        for n in range(chunks)
    ]
    for n in range(1, chunks):
        query_out(n)
    q_copies[0].start()

    for n in range(tiles):
        loads[s_base + n].wait()
        hid_v[:, n * 256:(n + 1) * 256] = jnp.dot(tok_v[...], same_v[n], preferred_element_type=F32).astype(BF16)
    k, v, tail = key_value()
    kv_mine[0:rows] = k
    kv_mine[rows:2 * rows] = v
    kv_mine[2 * rows:] = tail
    for n in range(chunks):
        q = jnp.dot(hid_v[...], query_v[n], preferred_element_type=F32)
        qa_v[n, 0:rows] = q[:, :128]
        qa_v[n, rows:] = q[:, 128:]

    kv_copy.wait_recv()
    kv_all[0, 0] = (kv_mine[...] + kv_in[...].astype(F32)).astype(BF16)

    ring = {}
    for n, (slot, l) in enumerate(SENDS):
        ring[slot, l] = pltpu.make_async_remote_copy(
            src_ref=kv_all.at[slot, 0], dst_ref=kv_all.at[slot ^ l, 0],
            send_sem=ring_send.at[n], recv_sem=ring_recv.at[slot ^ l],
            device_id=link[l], device_id_type=MESH,
        )
    came = {slot ^ l: copy for (slot, l), copy in ring.items()}
    cores = {
        slot: pltpu.make_async_remote_copy(
            src_ref=kv_all.at[slot, 0], dst_ref=kv_all.at[slot, 1],
            send_sem=core_send.at[slot], recv_sem=core_recv.at[slot],
            device_id=other, device_id_type=MESH,
        )
        for slot in range(8)
    }

    def unpack(place, slot):
        lane = lax.broadcasted_iota(jnp.int32, (half, 128), 1)
        for c in range(2):
            at = c * rows
            keys_v[place, at:at + rows] = kv_all[slot, c, 0:rows]
            vals_v[place, at:at + rows, 0:128] = kv_all[slot, c, rows:2 * rows]
            t = kv_all[slot, c, 2 * rows:].astype(F32)
            ones = jnp.where(lane == dv - 128, 1.0, 0.0)
            first = jnp.where(lane < dv - 128, t, ones)
            second = jnp.where(lane < dv - 128, pltpu.roll(t, 64, 1), ones)
            vals_v[place, at:at + half, 128:256] = first.astype(BF16)
            vals_v[place, at + half:at + rows, 128:256] = second.astype(BF16)

    def arrive(slot):
        came[slot].wait_recv()
        cores[slot].start()

    def stage(place):
        slot = ORDER[place]
        if place == 1:
            arrive(Y)
            ring[Y, H].start()
            arrive(M)
            ring[M, Y].start()
            ring[M, H].start()
            arrive(H)
            q_copies[2].start()
        if place == 4:
            arrive(Y ^ M)
            ring[Y ^ M, H].start()
            arrive(Y ^ H)
            q_copies[3].start()
        if place == 5:
            arrive(M ^ H)
        if place == 7:
            arrive(Y ^ M ^ H)
        cores[slot].wait_recv()
        unpack(place, slot)

    ring[0, Y].start()
    ring[0, M].start()
    ring[0, H].start()
    cores[0].start()
    q_copies[1].start()
    loads[o_base].wait()

    scale = dk ** -0.5 * math.log2(math.e)
    q_rows = 2 * rows
    step_keys = 2 * rows

    def chunk(c, carry):
        for n in range(chunks):
            @pl.when(c == n)
            def _():
                q_copies[n].wait_recv()
        q_v[...] = ((qa_v[c] + qb_in[c].astype(F32)) * scale).astype(BF16)
        peak_v[...] = jnp.full_like(peak_v, -jnp.inf)
        acc_v[...] = jnp.zeros_like(acc_v)

        def step(place, carry):
            for n in range(8):
                @pl.when((c == 0) & (place == n))
                def _():
                    stage(n)
            q = q_v[...]
            peak = peak_v[:, 0:1]
            acc = acc_v[...]
            for j in range(0, step_keys, 256):
                s = lax.dot_general(q, keys_v[place, j:j + 256], NT, preferred_element_type=F32)
                new = jnp.maximum(peak, jnp.max(s, axis=1, keepdims=True))
                weights = jnp.exp2(s - new).astype(BF16)
                acc = acc * jnp.exp2(peak - new) + jnp.dot(
                    weights, vals_v[place, j:j + 256], preferred_element_type=F32
                )
                peak = new
            peak_v[...] = jnp.broadcast_to(peak, peak_v.shape)
            acc_v[...] = acc
            return carry

        lax.fori_loop(0, 8, step, 0)
        total = acc_v[:, dv:dv + 1]
        for h in range(2):
            at = h * rows
            mixed = (acc_v[at:at + rows, 0:dv] / total[at:at + rows]).astype(BF16)
            w = out_v[pl.ds(pl.multiple_of((2 * c + h) * dv, dv), dv), :]
            part = jnp.dot(mixed, w, preferred_element_type=F32)
            if h == 0:
                first = part
        both = first + part

        @pl.when(c == 0)
        def _():
            sum_v[...] = both

        @pl.when(c > 0)
        def _():
            sum_v[...] += both
        return carry

    lax.fori_loop(0, chunks, chunk, 0)
    out_ref[0] = sum_v[...].astype(BF16)

    kv_copy.wait_send()
    for copy in q_copies:
        copy.wait_send()
    for copy in ring.values():
        copy.wait_send()
    for copy in cores.values():
        copy.wait_send()


def body(tokens, w_same, w_partner, w_query, w_key, w_value, w_out):
    _, rows, width = tokens.shape
    dk, dv = w_key.shape[1], w_value.shape[1]
    heads = w_query.shape[1] // dk
    chunks, tiles, pack = heads // 2, width // 256, 2 * rows + rows // 2
    dma = pltpu.SemaphoreType.DMA
    anyspace = pl.BlockSpec(memory_space=pl.ANY)
    return pl.pallas_call(
        functools.partial(kernel, (rows, width, heads, dk, dv)),
        out_shape=jax.ShapeDtypeStruct((1, rows, width), BF16),
        in_specs=[anyspace] * 7,
        out_specs=pl.BlockSpec(memory_space=pltpu.VMEM),
        scratch_shapes=[
            pltpu.VMEM((rows, width), BF16),
            pltpu.VMEM((rows, width), BF16),
            pltpu.VMEM((tiles, width, 256), BF16),
            pltpu.VMEM((tiles, width, 256), BF16),
            pltpu.VMEM((chunks, width, 256), BF16),
            pltpu.VMEM((width, dk), BF16),
            pltpu.VMEM((256, width), BF16),
            pltpu.VMEM((heads * dv, width), BF16),
            pltpu.VMEM((rows, width), BF16),
            pltpu.VMEM((pack, 128), BF16),
            pltpu.VMEM((pack, 128), BF16),
            pltpu.VMEM((pack, 128), F32),
            pltpu.VMEM((8, 2, pack, 128), BF16),
            pltpu.VMEM((8, 2 * rows, 128), BF16),
            pltpu.VMEM((8, 2 * rows, 256), BF16),
            pltpu.VMEM((chunks, 2 * rows, 128), BF16),
            pltpu.VMEM((chunks, 2 * rows, 128), BF16),
            pltpu.VMEM((chunks, 2 * rows, 128), F32),
            pltpu.VMEM((2 * rows, 128), BF16),
            pltpu.VMEM((2 * rows, 128), F32),
            pltpu.VMEM((2 * rows, 256), F32),
            pltpu.VMEM((rows, width), F32),
            dma((1 + 2 * tiles + 3 + chunks + 1,)),
            dma((1 + chunks,)),
            dma((1 + chunks,)),
            dma((len(SENDS),)),
            dma((8,)),
            dma((8,)),
            dma((8,)),
        ],
        compiler_params=pltpu.CompilerParams(
            collective_id=0, has_side_effects=True, vmem_limit_bytes=62 << 20
        ),
        name="strand_attention",
    )(tokens, w_same, w_partner, w_query, w_key, w_value.T, w_out)


def solution(mesh):
    placed = (P("ws", "seq", None), P(), P(), P(), P(), P(), P())
    return jax.shard_map(
        body, mesh=mesh, in_specs=placed, out_specs=P("ws", "seq", None), check_vma=False
    )
```

time: 285 us -> 146 us (0.51)
  Pallas kernels: 0 us -> 144 us
  waiting for transfers between devices: 127 us -> 0 us
  matrix products: 82.3 us -> 0 us
  local copies, waits for them, and re-layouts: 27 us -> 2.36 us
  other arithmetic: 23.8 us -> 0 us
  between operations: 13.5 us -> 0.01 us
  starting transfers between devices: 9.18 us -> 0 us
    pallas_call x0 -> x1, Pallas kernels: none -> 144 us  [body(): pl.pallas_call(functools.partial(kernel, (rows, width, heads, dk, dv)), o...]
    ppermute x5 -> x0, waiting for transfers between devices: 97.5 us -> none  [swapped(): return lax.ppermute(value, axis, pairs)]
    dot_general x8 -> x0, matrix products: 82.3 us -> none  [the longest x1 29.3 us: body(): lax.dot_general(query_rows, lax.all_gather(keys, 'seq', axis=0, tiled=Tru...]
    all_gather x2 -> x0, waiting for transfers between devices: 29.3 us -> none  [the longest x1 29.2 us: body(): lax.all_gather(keys, 'seq', axis=0, tiled=True)]
    reduce_sum x1 -> x0, other arithmetic: 23.8 us -> none  [body(): total = total * decay + jnp.sum(weights, axis=1)]
    rev x1 -> x0, local copies, waits for them, and re-layouts: 17.4 us -> none  [body(): mirrored = jnp.flip(partner[0], 0)]
    ppermute x5 -> x0, starting transfers between devices: 8.96 us -> none  [swapped(): return lax.ppermute(value, axis, pairs)]
    reshape x2 -> x0, local copies, waits for them, and re-layouts: 5.96 us -> none  [the longest x1 3.75 us: body(): (accum / total[:, None]).astype(jnp.bfloat16)]
  transfers between devices with their start and end apart: 7 -> 0, of which waited for: 6 -> 0; matrix products, arithmetic and copies ran while one was open for 24% -> 0% of each run, Pallas kernels for 0% -> 0%
where the time goes in v1:
time: 146 us
  Pallas kernels  144 us (99%)
  local copies, waits for them, and re-layouts  2.36 us (2%)
    pallas_call x1, Pallas kernels, body(): pl.pallas_call(functools.partial(kernel, (rows, width, heads, dk, dv)), o...  144 us

profile of v1, /device:TPU:1, one launch (start us, length us, event | category | flops | bytes accessed | tf_op | source)
XLA Modules:
  0.0 146.2 jit_solution(16505647633910297575)
XLA Ops:
  0.0 143.8 %strand_attention.1 = bf16[1,384,1536]{2,1,0:T(8,128)(2,1)} custom-call(bf16[1,384,1536]{2,1,0:T(8,128)(2,1)} %tok.1, bf16[1536,1536]{1,0:T(8,128)(2,1)} %w_same.1, bf16[1536,1536]{1,0:T(8,128)(2,1)} %w_partner.1, bf16[1536,1024]{1,0:T(8,128)(2,1)} %w_query.1, bf16[1536,128]{1,0:T(8,128)(2,1)} %w_key.1, bf16[192,1536]{1,0:T(8,128)(2,1)} %bitcast.1, ...), custom_call_target="tpu_custom_call" | custom-call | tf_op jit(solution)/shard_map/strand_attention/pallas_call | solution.py:273
  143.8 2.4 %copy.9 = bf16[1,384,1536]{2,1,0:T(8,128)(2,1)} copy(bf16[1,384,1536]{2,1,0:T(8,128)(2,1)} %strand_attention.1) | data formatting | bytes 2359296

commit v2 on v0

v2 whole, which is shorter than its diff:
```python
import functools
import math

import jax
import jax.numpy as jnp
from jax import lax
from jax.experimental import pallas as pl
from jax.experimental.pallas import tpu as pltpu
from jax.sharding import PartitionSpec as P

MESH = pl.DeviceIdType.MESH
F32 = jnp.float32
BF16 = jnp.bfloat16
NT = (((1,), (1,)), ((), ()))
VMEM_LIMIT = 50 << 20
PIECE = 512

Y, H, M = 1, 2, 4
ORDER = (0, H, Y, M, Y ^ H, M ^ H, Y ^ M, Y ^ M ^ H)
PLACE = {slot: place for place, slot in enumerate(ORDER)}
SENDS = ((0, H, 0, 2), (0, Y, 0, 2), (0, M, 0, 2), (Y, H, 0, 2), (M, H, 0, 2), (M, Y, 0, 1), (Y, M, 1, 2), (Y ^ M, H, 0, 2))


def kernel(
    dims,
    tok, w_same, w_partner, w_query, w_key, w_value_t,
    out_ref,
    tok_v, same_v, partner_v, query_v, key_v, value_v, hid_v,
    kv_out, kv_in, kv_mine, kv_all, keys_v, vals_v,
    qb_out, qb_in, qa_v, q_v, peak_v, acc_v,
    load_sem, pair_send, pair_recv, ring_send, ring_recv, core_send, core_recv,
):
    rows, width, heads, dk, dv = dims
    chunks = heads // 2
    half = rows // 2
    pack = 2 * rows + half
    ws = lax.axis_index("ws")
    seq = lax.axis_index("seq")
    last = lax.axis_size("seq") - 1
    x, y, core = seq // 4, (seq // 2) % 2, seq % 2
    pair = {"ws": ws + 1 - 2 * (ws % 2), "seq": last - seq}
    other = {"ws": ws, "seq": seq + 1 - 2 * core}
    link = {
        Y: {"ws": ws, "seq": seq + 2 - 4 * y},
        H: {"ws": ws, "seq": seq + 4 - 8 * (x % 2)},
        M: {"ws": ws, "seq": (3 - x) * 4 + y * 2 + core},
    }

    tiles = width // PIECE
    tail_rows = dv - 128
    sources = [(tok.at[0], tok_v)]
    sources += [(w_partner.at[:, pl.ds(n * PIECE, PIECE)], partner_v.at[n]) for n in range(tiles)]
    sources += [
        (w_key, key_v),
        (w_value_t, value_v.at[pl.ds(0, dv)]),
        (w_value_t.at[pl.ds(128, tail_rows)], value_v.at[pl.ds(dv, tail_rows)]),
    ]
    sources += [(w_query, query_v), (w_same, same_v)]
    loads = [pltpu.make_async_copy(src, dst, load_sem.at[n]) for n, (src, dst) in enumerate(sources)]
    kv_base = 1 + tiles
    q_base = kv_base + 3
    s_base = q_base + 1

    def begin(first, stop):
        for copy in loads[first:stop]:
            copy.start()

    begin(0, q_base)
    barrier = pltpu.get_barrier_semaphore()
    for peer in (pair, other, link[Y], link[H], link[M]):
        pl.semaphore_signal(barrier, inc=1, device_id=peer, device_id_type=MESH)

    turned = lax.broadcasted_iota(jnp.int32, (rows, rows), 0) + lax.broadcasted_iota(jnp.int32, (rows, rows), 1)
    turn = jnp.where(turned == rows - 1, 1.0, 0.0).astype(BF16)

    def key_value():
        h = hid_v[...]
        k = jnp.dot(h, key_v[...], preferred_element_type=F32)
        v = lax.dot_general(h, value_v[...], NT, preferred_element_type=F32)
        return k, v

    def tail(v):
        lane = lax.broadcasted_iota(jnp.int32, (half, 128), 1)
        return jnp.where(lane < tail_rows, v[:half, 128:], v[half:, 128:])

    with jax.named_scope("w_tok"):
        loads[0].wait()
    with jax.named_scope("hB"):
        for n in range(tiles):
            loads[1 + n].wait()
            part = jnp.dot(tok_v[...], partner_v[n], preferred_element_type=F32)
            hid_v[:, n * PIECE:(n + 1) * PIECE] = part.astype(BF16)
            if n == 0:
                begin(q_base, s_base)
    begin(s_base, len(loads))
    with jax.named_scope("kvB"):
        for n in range(3):
            loads[kv_base + n].wait()
        k, v = key_value()
        both = jnp.concatenate([k, v], axis=1).astype(BF16)
        both = jnp.dot(turn, both, preferred_element_type=F32)
        kv_out[0:rows] = both[:, 0:128].astype(BF16)
        kv_out[rows:2 * rows] = both[:, 128:256].astype(BF16)
        kv_out[2 * rows:] = tail(both[:, 128:]).astype(BF16)

    kv_copy = pltpu.make_async_remote_copy(
        src_ref=kv_out, dst_ref=kv_in, send_sem=pair_send.at[0], recv_sem=pair_recv.at[0],
        device_id=pair, device_id_type=MESH,
    )
    q_copies = [
        pltpu.make_async_remote_copy(
            src_ref=qb_out.at[n], dst_ref=qb_in.at[n], send_sem=pair_send.at[1 + n], recv_sem=pair_recv.at[1 + n],
            device_id=pair, device_id_type=MESH,
        )
        for n in range(chunks)
    ]
    with jax.named_scope("barrier"):
        pl.semaphore_wait(barrier, 5)
    kv_copy.start()

    def heads_of(q):
        for n in range(heads):
            at = (n % 2) * rows
            yield n // 2, slice(at, at + rows), q[:, n * dk:(n + 1) * dk]

    with jax.named_scope("qB"):
        loads[q_base].wait()
        q = jnp.dot(hid_v[...], query_v[...], preferred_element_type=F32).astype(BF16)
        q = jnp.dot(turn, q, preferred_element_type=F32).astype(BF16)
        for n, at, part in heads_of(q):
            qb_out[n, at] = part

    with jax.named_scope("hA"):
        loads[s_base].wait()
        q_copies[0].start()
        hid_v[...] = jnp.dot(tok_v[...], same_v[...], preferred_element_type=F32).astype(BF16)
    with jax.named_scope("kvA"):
        k, v = key_value()
        kv_mine[0:rows] = k
        kv_mine[rows:2 * rows] = v[:, :128]
        kv_mine[2 * rows:] = tail(v)
    with jax.named_scope("qA"):
        q = jnp.dot(hid_v[...], query_v[...], preferred_element_type=F32)
        for n, at, part in heads_of(q):
            qa_v[n, at] = part

    with jax.named_scope("w_kv"):
        kv_copy.wait_recv()
    kv_all[0, 0] = (kv_mine[...] + kv_in[...].astype(F32)).astype(BF16)

    ring, came = {}, {slot: [] for slot in range(8)}
    for n, (slot, l, first, stop) in enumerate(SENDS):
        part = pl.ds(first * pack // 2, (stop - first) * pack // 2)
        ring[slot, l] = pltpu.make_async_remote_copy(
            src_ref=kv_all.at[slot, 0, part], dst_ref=kv_all.at[slot ^ l, 0, part],
            send_sem=ring_send.at[n], recv_sem=ring_recv.at[n],
            device_id=link[l], device_id_type=MESH,
        )
        came[slot ^ l].append(ring[slot, l])
    cores = {
        slot: pltpu.make_async_remote_copy(
            src_ref=kv_all.at[slot, 0], dst_ref=kv_all.at[slot, 1],
            send_sem=core_send.at[slot], recv_sem=core_recv.at[slot],
            device_id=other, device_id_type=MESH,
        )
        for slot in range(8)
    }

    def unpack(slot, c):
        place = PLACE[slot]
        lane = lax.broadcasted_iota(jnp.int32, (half, 128), 1)
        at = c * rows
        keys_v[place, at:at + rows] = kv_all[slot, c, 0:rows]
        vals_v[place, at:at + rows, 0:128] = kv_all[slot, c, rows:2 * rows]
        t = kv_all[slot, c, 2 * rows:].astype(F32)
        ones = jnp.where(lane == tail_rows, 1.0, 0.0)
        first = jnp.where(lane < tail_rows, t, ones)
        second = jnp.where(lane < tail_rows, pltpu.roll(t, 64, 1), ones)
        vals_v[place, at:at + half, 128:256] = first.astype(BF16)
        vals_v[place, at + half:at + rows, 128:256] = second.astype(BF16)

    def arrive(slot, *onward):
        with jax.named_scope(f"w_slot{slot}"):
            for copy in came[slot]:
                copy.wait_recv()
        cores[slot].start()
        for l in onward:
            ring[slot, l].start()
        unpack(slot, 0)

    def complete(slot):
        with jax.named_scope(f"w_core{slot}"):
            cores[slot].wait_recv()
        unpack(slot, 1)

    def stage(place):
        if place == 1:
            arrive(H)
            arrive(Y, H)
            arrive(M, H)
            q_copies[2].start()
            ring[M, Y].start()
            ring[Y, M].start()
            q_copies[3].start()
        complete(ORDER[place])

    scale = dk ** -0.5 * math.log2(math.e)

    def query(c):
        for n in range(chunks):
            @pl.when(c == n)
            def _():
                with jax.named_scope(f"w_q{n}"):
                    q_copies[n].wait_recv()
        q_v[c] = ((qa_v[c] + qb_in[c].astype(F32)) * scale).astype(BF16)

    def attend(q, places, peak, acc):
        for place in places:
            for j in range(0, 2 * rows, 256):
                s = lax.dot_general(q, keys_v[place, j:j + 256], NT, preferred_element_type=F32)
                new = jnp.maximum(peak, jnp.broadcast_to(jnp.max(s, axis=1, keepdims=True), peak.shape))
                weights = jnp.concatenate([jnp.exp2(s[:, :128] - new), jnp.exp2(s[:, 128:] - new)], axis=1).astype(BF16)
                keep = jnp.exp2(peak - new)
                acc = acc * jnp.concatenate([keep, keep], axis=1) + jnp.dot(
                    weights, vals_v[place, j:j + 256], preferred_element_type=F32
                )
                peak = new
        return peak, acc

    unpack(0, 0)
    ring[0, H].start()
    ring[0, Y].start()
    ring[0, M].start()
    cores[0].start()
    q_copies[1].start()

    query(0)
    peak_v[0] = jnp.full(peak_v.shape[1:], -jnp.inf, F32)
    acc_v[0] = jnp.zeros(acc_v.shape[1:], F32)

    def early(place, carry):
        for n in range(4):
            @pl.when(place == n)
            def _():
                stage(n)
        with jax.named_scope("early"):
            peak_v[0], acc_v[0] = attend(q_v[0], (place,), peak_v[0], acc_v[0])
        return carry

    lax.fori_loop(0, 4, early, 0)

    def near(c, carry):
        query(c)
        with jax.named_scope("near"):
            start = jnp.full(peak_v.shape[1:], -jnp.inf, F32), jnp.zeros(acc_v.shape[1:], F32)
            peak_v[c], acc_v[c] = attend(q_v[c], range(4), *start)
        return carry

    lax.fori_loop(1, chunks - 1, near, 0)

    arrive(Y ^ H)
    arrive(M ^ H)
    complete(Y ^ H)
    complete(M ^ H)

    def middle(c, carry):
        with jax.named_scope("mid"):
            peak_v[c], acc_v[c] = attend(q_v[c], (4, 5), peak_v[c], acc_v[c])
        return carry

    lax.fori_loop(0, chunks - 1, middle, 0)
    arrive(Y ^ M, H)
    near(chunks - 1, 0)
    complete(Y ^ M)

    def store(c, acc):
        mixed = acc * (1.0 / acc[:, dv:dv + 1])
        lane = lax.broadcasted_iota(jnp.int32, (rows, 128), 1)
        a, b = mixed[:rows], mixed[rows:]
        turned_b = pltpu.roll(b[:, :128], 64, 1)
        inner = jnp.where(lane < 64, a[:, 128:], turned_b)
        end = jnp.where(lane < 64, turned_b, pltpu.roll(b[:, 128:], 64, 1))
        at = pl.multiple_of(c * 2 * dv, 128)
        out_ref[:, pl.ds(at, 2 * dv)] = jnp.concatenate([a[:, :128], inner, end], axis=1).astype(BF16)

    def far(k, carry):
        c = (k + chunks - 1) % chunks
        place = 4 + 2 * ((k + chunks - 1) // chunks)

        @pl.when(k == 1)
        def _():
            arrive(Y ^ M ^ H)
            complete(Y ^ M ^ H)

        with jax.named_scope("far"):
            peak_v[c], acc_v[c] = attend(q_v[c], (place, place + 1), peak_v[c], acc_v[c])

        @pl.when(k > 0)
        def _():
            store(c, acc_v[c])
        return carry

    lax.fori_loop(0, chunks + 1, far, 0)

    kv_copy.wait_send()
    for copy in q_copies:
        copy.wait_send()
    for copy in ring.values():
        copy.wait_send()
    for copy in cores.values():
        copy.wait_send()


def body(tokens, w_same, w_partner, w_query, w_key, w_value, w_out):
    _, rows, width = tokens.shape
    dk, dv = w_key.shape[1], w_value.shape[1]
    heads = w_query.shape[1] // dk
    chunks, tiles, pack = heads // 2, width // PIECE, 2 * rows + rows // 2
    dma = pltpu.SemaphoreType.DMA
    in_hbm = pl.BlockSpec(memory_space=pltpu.HBM)
    mixed = pl.pallas_call(
        functools.partial(kernel, (rows, width, heads, dk, dv)),
        out_shape=jax.ShapeDtypeStruct((rows, heads * dv), BF16),
        in_specs=[in_hbm] * 6,
        out_specs=pl.BlockSpec(memory_space=pltpu.VMEM),
        scratch_shapes=[
            pltpu.VMEM((rows, width), BF16),
            pltpu.VMEM((width, width), BF16),
            pltpu.VMEM((tiles, width, PIECE), BF16),
            pltpu.VMEM((width, heads * dk), BF16),
            pltpu.VMEM((width, dk), BF16),
            pltpu.VMEM((256, width), BF16),
            pltpu.VMEM((rows, width), BF16),
            pltpu.VMEM((pack, 128), BF16),
            pltpu.VMEM((pack, 128), BF16),
            pltpu.VMEM((pack, 128), F32),
            pltpu.VMEM((8, 2, pack, 128), BF16),
            pltpu.VMEM((8, 2 * rows, 128), BF16),
            pltpu.VMEM((8, 2 * rows, 256), BF16),
            pltpu.VMEM((chunks, 2 * rows, 128), BF16),
            pltpu.VMEM((chunks, 2 * rows, 128), BF16),
            pltpu.VMEM((chunks, 2 * rows, 128), F32),
            pltpu.VMEM((chunks, 2 * rows, 128), BF16),
            pltpu.VMEM((chunks, 2 * rows, 128), F32),
            pltpu.VMEM((chunks, 2 * rows, 256), F32),
            dma((1 + tiles + 5,)),
            dma((1 + chunks,)),
            dma((1 + chunks,)),
            dma((len(SENDS),)),
            dma((len(SENDS),)),
            dma((8,)),
            dma((8,)),
        ],
        compiler_params=pltpu.CompilerParams(
            collective_id=0, has_side_effects=True, vmem_limit_bytes=VMEM_LIMIT
        ),
        name="strand_attention",
    )(*(pltpu.with_memory_space_constraint(a, pltpu.HBM) for a in (tokens, w_same, w_partner, w_query, w_key, w_value.T)))
    return jnp.dot(mixed, w_out, preferred_element_type=F32).astype(BF16)[None]


def solution(mesh):
    placed = (P("ws", "seq", None), P(), P(), P(), P(), P(), P())
    return jax.shard_map(
        body, mesh=mesh, in_specs=placed, out_specs=P("ws", "seq", None), check_vma=False
    )
```

time: 285 us -> 65.2 us (0.23)
  waiting for transfers between devices: 127 us -> 0 us
  matrix products: 82.3 us -> 3 us
  Pallas kernels: 0 us -> 62 us
  local copies, waits for them, and re-layouts: 27 us -> 0.01 us
  other arithmetic: 23.8 us -> 0 us
  between operations: 13.5 us -> 0.02 us
  starting transfers between devices: 9.18 us -> 0 us
    ppermute x5 -> x0, waiting for transfers between devices: 97.5 us -> none  [swapped(): return lax.ppermute(value, axis, pairs)]
    dot_general x8 -> x1, matrix products: 82.3 us -> 3 us  [body(): return jnp.dot(mixed, w_out, preferred_element_type=F32).astype(BF16)[None]]
    pallas_call x0 -> x1, Pallas kernels: none -> 62 us  [body(): pl.pallas_call(functools.partial(kernel, (rows, width, heads, dk, dv)), o...]
    all_gather x2 -> x0, waiting for transfers between devices: 29.3 us -> none  [the longest x1 29.2 us: body(): lax.all_gather(keys, 'seq', axis=0, tiled=True)]
    reduce_sum x1 -> x0, other arithmetic: 23.8 us -> none  [body(): total = total * decay + jnp.sum(weights, axis=1)]
    rev x1 -> x0, local copies, waits for them, and re-layouts: 17.4 us -> none  [body(): mirrored = jnp.flip(partner[0], 0)]
    ppermute x5 -> x0, starting transfers between devices: 8.96 us -> none  [swapped(): return lax.ppermute(value, axis, pairs)]
    reshape x2 -> x0, local copies, waits for them, and re-layouts: 5.96 us -> none  [the longest x1 3.75 us: body(): (accum / total[:, None]).astype(jnp.bfloat16)]
  transfers between devices with their start and end apart: 7 -> 0, of which waited for: 6 -> 0; matrix products, arithmetic and copies ran while one was open for 24% -> 0% of each run, Pallas kernels for 0% -> 0%
where the time goes in v2:
time: 65.2 us; the launch traced here: 65.1 us
  Pallas kernels  62 us (95%)
  matrix products  3 us (5%)
    pallas_call x1, Pallas kernels, body(): pl.pallas_call(functools.partial(kernel, (rows, width, heads, dk, dv)), o...  62 us
    dot_general x1, matrix products, body(): return jnp.dot(mixed, w_out, preferred_element_type=F32).astype(BF16)[None]  3 us

profile of v2, /device:TPU:1, one launch (start us, length us, event | category | flops | bytes accessed | tf_op | source)
XLA Modules:
  0.0 65.1 jit_solution(4180777449619446190)
XLA Ops:
  0.0 0.0 copy-start
  0.0 62.0 %strand_attention.1 = bf16[384,1536]{1,0:T(8,128)(2,1)S(1)} custom-call(bf16[1,384,1536]{2,1,0:T(8,128)(2,1)} %tok.1, bf16[1536,1536]{1,0:T(8,128)(2,1)} %w_same.1, bf16[1536,1536]{1,0:T(8,128)(2,1)} %w_partner.1, bf16[1536,1024]{1,0:T(8,128)(2,1)} %w_query.1, bf16[1536,128]{1,0:T(8,128)(2,1)} %w_key.1, bf16[192,1536]{1,0:T(8,128)(2,1)} %bitcast.5), custom_call_target="tpu_custom_call" | custom-call | tf_op jit(solution)/shard_map/strand_attention/pallas_call | solution.py:321
  62.1 0.0 copy-done
  62.1 3.0 %fusion = bf16[1,384,1536]{2,1,0:T(8,128)(2,1)} fusion(bf16[384,1536]{1,0:T(8,128)(2,1)S(1)} %strand_attention.1, bf16[1536,1536]{1,0:T(8,128)(2,1)S(1)} %copy-done), kind=kOutput, calls=%fused_computation.1 | convolution fusion | flops 1812529152 | bytes 7077888 | tf_op jit(solution)/shard_map/dot_general | solution.py:359
Async XLA Ops:
  0.0 62.1 %copy-start = (bf16[1536,1536]{1,0:T(8,128)(2,1)S(1)}, bf16[1536,1536]{1,0:T(8,128)(2,1)}, u32[]{:S(2)}) copy-start(bf16[1536,1536]{1,0:T(8,128)(2,1)} %param.13) | copy-start | bytes 14155780

commit v3 on v2

--- a/solution.py
+++ b/solution.py
@@ -73,11 +73,11 @@
     turned = lax.broadcasted_iota(jnp.int32, (rows, rows), 0) + lax.broadcasted_iota(jnp.int32, (rows, rows), 1)
     turn = jnp.where(turned == rows - 1, 1.0, 0.0).astype(BF16)
 
-    def key_value():
-        h = hid_v[...]
-        k = jnp.dot(h, key_v[...], preferred_element_type=F32)
-        v = lax.dot_general(h, value_v[...], NT, preferred_element_type=F32)
-        return k, v
+    def key(h):
+        return jnp.dot(h, key_v[...], preferred_element_type=F32)
+
+    def value(h):
+        return lax.dot_general(h, value_v[...], NT, preferred_element_type=F32)
 
     def tail(v):
         lane = lax.broadcasted_iota(jnp.int32, (half, 128), 1)
@@ -93,30 +93,27 @@
             if n == 0:
                 begin(q_base, s_base)
     begin(s_base, len(loads))
-    with jax.named_scope("kvB"):
+    def to_pair(src, dst, n):
+        return pltpu.make_async_remote_copy(
+            src_ref=src, dst_ref=dst, send_sem=pair_send.at[n], recv_sem=pair_recv.at[n],
+            device_id=pair, device_id_type=MESH,
+        )
+
+    kv_parts = (pl.ds(0, rows), pl.ds(rows, pack - rows))
+    kv_copies = [to_pair(kv_out.at[part], kv_in.at[part], n) for n, part in enumerate(kv_parts)]
+    q_copies = [to_pair(qb_out.at[n], qb_in.at[n], 2 + n) for n in range(chunks)]
+    with jax.named_scope("kB"):
         for n in range(3):
             loads[kv_base + n].wait()
-        k, v = key_value()
-        both = jnp.concatenate([k, v], axis=1).astype(BF16)
-        both = jnp.dot(turn, both, preferred_element_type=F32)
-        kv_out[0:rows] = both[:, 0:128].astype(BF16)
-        kv_out[rows:2 * rows] = both[:, 128:256].astype(BF16)
-        kv_out[2 * rows:] = tail(both[:, 128:]).astype(BF16)
-
-    kv_copy = pltpu.make_async_remote_copy(
-        src_ref=kv_out, dst_ref=kv_in, send_sem=pair_send.at[0], recv_sem=pair_recv.at[0],
-        device_id=pair, device_id_type=MESH,
-    )
-    q_copies = [
-        pltpu.make_async_remote_copy(
-            src_ref=qb_out.at[n], dst_ref=qb_in.at[n], send_sem=pair_send.at[1 + n], recv_sem=pair_recv.at[1 + n],
-            device_id=pair, device_id_type=MESH,
-        )
-        for n in range(chunks)
-    ]
+        kv_out[0:rows] = key(hid_v[...]).astype(BF16)
     with jax.named_scope("barrier"):
         pl.semaphore_wait(barrier, 5)
-    kv_copy.start()
+    kv_copies[0].start()
+    with jax.named_scope("vB"):
+        v = value(hid_v[...])
+        kv_out[rows:2 * rows] = v[:, :128].astype(BF16)
+        kv_out[2 * rows:] = tail(v).astype(BF16)
+    kv_copies[1].start()
 
     def heads_of(q):
         for n in range(heads):
@@ -135,8 +132,9 @@
         q_copies[0].start()
         hid_v[...] = jnp.dot(tok_v[...], same_v[...], preferred_element_type=F32).astype(BF16)
     with jax.named_scope("kvA"):
-        k, v = key_value()
-        kv_mine[0:rows] = k
+        turned_hid = jnp.dot(turn, hid_v[...], preferred_element_type=F32).astype(BF16)
+        kv_mine[0:rows] = key(turned_hid)
+        v = value(turned_hid)
         kv_mine[rows:2 * rows] = v[:, :128]
         kv_mine[2 * rows:] = tail(v)
     with jax.named_scope("qA"):
@@ -145,7 +143,8 @@
             qa_v[n, at] = part
 
     with jax.named_scope("w_kv"):
-        kv_copy.wait_recv()
+        for copy in kv_copies:
+            copy.wait_recv()
     kv_all[0, 0] = (kv_mine[...] + kv_in[...].astype(F32)).astype(BF16)
 
     ring, came = {}, {slot: [] for slot in range(8)}
@@ -167,9 +166,10 @@
     }
 
     def unpack(slot, c):
-        place = PLACE[slot]
+        place, at = PLACE[slot], c * rows
+        if slot in (Y, M):
+            place, at = 2 + c, rows * (slot == M)
         lane = lax.broadcasted_iota(jnp.int32, (half, 128), 1)
-        at = c * rows
         keys_v[place, at:at + rows] = kv_all[slot, c, 0:rows]
         vals_v[place, at:at + rows, 0:128] = kv_all[slot, c, rows:2 * rows]
         t = kv_all[slot, c, 2 * rows:].astype(F32)
@@ -194,24 +194,32 @@
         unpack(slot, 1)
 
     def stage(place):
+        if place == 0:
+            complete(0)
         if place == 1:
             arrive(H)
+            complete(H)
             arrive(Y, H)
             arrive(M, H)
-            q_copies[2].start()
             ring[M, Y].start()
             ring[Y, M].start()
             q_copies[3].start()
-        complete(ORDER[place])
+        if place == 3:
+            complete(Y)
+            complete(M)
 
     scale = dk ** -0.5 * math.log2(math.e)
 
     def query(c):
-        for n in range(chunks):
-            @pl.when(c == n)
-            def _():
-                with jax.named_scope(f"w_q{n}"):
-                    q_copies[n].wait_recv()
+        if isinstance(c, int):
+            with jax.named_scope(f'w_q{c}'):
+                q_copies[c].wait_recv()
+        else:
+            for n in range(2, chunks):
+                @pl.when(c == n)
+                def _():
+                    with jax.named_scope(f"w_q{n}"):
+                        q_copies[n].wait_recv()
         q_v[c] = ((qa_v[c] + qb_in[c].astype(F32)) * scale).astype(BF16)
 
     def attend(q, places, peak, acc):
@@ -233,6 +241,7 @@
     ring[0, M].start()
     cores[0].start()
     q_copies[1].start()
+    q_copies[2].start()
 
     query(0)
     peak_v[0] = jnp.full(peak_v.shape[1:], -jnp.inf, F32)
@@ -249,29 +258,46 @@
 
     lax.fori_loop(0, 4, early, 0)
 
-    def near(c, carry):
-        query(c)
+    def one(c, place):
+        with jax.named_scope("one"):
+            peak_v[c], acc_v[c] = attend(q_v[c], (place,), peak_v[c], acc_v[c])
+
+    def begin_chunk(c, places):
         with jax.named_scope("near"):
             start = jnp.full(peak_v.shape[1:], -jnp.inf, F32), jnp.zeros(acc_v.shape[1:], F32)
-            peak_v[c], acc_v[c] = attend(q_v[c], range(4), *start)
+            peak_v[c], acc_v[c] = attend(q_v[c], places, *start)
+
+    def second(c, carry):
+        one(c, PLACE[Y ^ H])
         return carry
 
-    lax.fori_loop(1, chunks - 1, near, 0)
-
+    def late(c, carry):
+        query(c)
+
+        @pl.when(c == chunks - 2)
+        def _():
+            complete(Y ^ H)
+
+        begin_chunk(c, range(5))
+
+        @pl.when(c == chunks - 2)
+        def _():
+            arrive(Y ^ M, H)
+            arrive(M ^ H)
+            lax.fori_loop(0, chunks - 2, second, 0)
+        return carry
+
+    query(1)
+    begin_chunk(1, range(4))
     arrive(Y ^ H)
-    arrive(M ^ H)
-    complete(Y ^ H)
+    lax.fori_loop(2, chunks, late, 0)
     complete(M ^ H)
-
-    def middle(c, carry):
-        with jax.named_scope("mid"):
-            peak_v[c], acc_v[c] = attend(q_v[c], (4, 5), peak_v[c], acc_v[c])
-        return carry
-
-    lax.fori_loop(0, chunks - 1, middle, 0)
-    arrive(Y ^ M, H)
-    near(chunks - 1, 0)
     complete(Y ^ M)
+    arrive(Y ^ M ^ H)
+    with jax.named_scope("two"):
+        peak_v[0], acc_v[0] = attend(q_v[0], (5, 6), peak_v[0], acc_v[0])
+    complete(Y ^ M ^ H)
+    one(0, 7)
 
     def store(c, acc):
         mixed = acc * (1.0 / acc[:, dv:dv + 1])
@@ -283,27 +309,16 @@
         at = pl.multiple_of(c * 2 * dv, 128)
         out_ref[:, pl.ds(at, 2 * dv)] = jnp.concatenate([a[:, :128], inner, end], axis=1).astype(BF16)
 
-    def far(k, carry):
-        c = (k + chunks - 1) % chunks
-        place = 4 + 2 * ((k + chunks - 1) // chunks)
-
-        @pl.when(k == 1)
-        def _():
-            arrive(Y ^ M ^ H)
-            complete(Y ^ M ^ H)
-
+    def far(c, carry):
         with jax.named_scope("far"):
-            peak_v[c], acc_v[c] = attend(q_v[c], (place, place + 1), peak_v[c], acc_v[c])
-
-        @pl.when(k > 0)
-        def _():
-            store(c, acc_v[c])
+            store(c - 1, acc_v[c - 1])
+            _, acc_v[c] = attend(q_v[c], range(5, 8), peak_v[c], acc_v[c])
         return carry
 
-    lax.fori_loop(0, chunks + 1, far, 0)
-
-    kv_copy.wait_send()
-    for copy in q_copies:
+    lax.fori_loop(1, chunks, far, 0)
+    store(chunks - 1, acc_v[chunks - 1])
+
+    for copy in kv_copies + q_copies:
         copy.wait_send()
     for copy in ring.values():
         copy.wait_send()
@@ -344,8 +359,8 @@
             pltpu.VMEM((chunks, 2 * rows, 128), F32),
             pltpu.VMEM((chunks, 2 * rows, 256), F32),
             dma((1 + tiles + 5,)),
-            dma((1 + chunks,)),
-            dma((1 + chunks,)),
+            dma((2 + chunks,)),
+            dma((2 + chunks,)),
             dma((len(SENDS),)),
             dma((len(SENDS),)),
             dma((8,)),

time: 65.2 us -> 60.1 us (0.922)
  Pallas kernels: 62 us -> 57 us
    pallas_call x1, Pallas kernels: 62 us -> 57 us  [body(): pl.pallas_call(functools.partial(kernel, (rows, width, heads, dk, dv)), o...]
where the time goes in v3:
time: 60.1 us; the launch traced here: 60 us
  Pallas kernels  57 us (95%)
  matrix products  3 us (5%)
    pallas_call x1, Pallas kernels, body(): pl.pallas_call(functools.partial(kernel, (rows, width, heads, dk, dv)), o...  57 us
    dot_general x1, matrix products, body(): return jnp.dot(mixed, w_out, preferred_element_type=F32).astype(BF16)[None]  3 us

profile of v3, /device:TPU:1, one launch (start us, length us, event | category | flops | bytes accessed | tf_op | source)
XLA Modules:
  0.0 60.0 jit_solution(18058547215496546668)
XLA Ops:
  0.0 0.0 copy-start
  0.0 57.0 %strand_attention.1 = bf16[384,1536]{1,0:T(8,128)(2,1)S(1)} custom-call(bf16[1,384,1536]{2,1,0:T(8,128)(2,1)} %tok.1, bf16[1536,1536]{1,0:T(8,128)(2,1)} %w_same.1, bf16[1536,1536]{1,0:T(8,128)(2,1)} %w_partner.1, bf16[1536,1024]{1,0:T(8,128)(2,1)} %w_query.1, bf16[1536,128]{1,0:T(8,128)(2,1)} %w_key.1, bf16[192,1536]{1,0:T(8,128)(2,1)} %bitcast.5), custom_call_target="tpu_custom_call" | custom-call | tf_op jit(solution)/shard_map/strand_attention/pallas_call | solution.py:336
  57.0 0.0 copy-done
  57.0 3.0 %fusion = bf16[1,384,1536]{2,1,0:T(8,128)(2,1)} fusion(bf16[384,1536]{1,0:T(8,128)(2,1)S(1)} %strand_attention.1, bf16[1536,1536]{1,0:T(8,128)(2,1)S(1)} %copy-done), kind=kOutput, calls=%fused_computation.1 | convolution fusion | flops 1812529152 | bytes 7077888 | tf_op jit(solution)/shard_map/dot_general | solution.py:374
Async XLA Ops:
  0.0 57.0 %copy-start = (bf16[1536,1536]{1,0:T(8,128)(2,1)S(1)}, bf16[1536,1536]{1,0:T(8,128)(2,1)}, u32[]{:S(2)}) copy-start(bf16[1536,1536]{1,0:T(8,128)(2,1)} %param.13) | copy-start | bytes 14155780

commit v4 on v3

--- a/solution.py
+++ b/solution.py
@@ -14,6 +14,7 @@
 NT = (((1,), (1,)), ((), ()))
 VMEM_LIMIT = 50 << 20
 PIECE = 512
+EARLY = 32
 
 Y, H, M = 1, 2, 4
 ORDER = (0, H, Y, M, Y ^ H, M ^ H, Y ^ M, Y ^ M ^ H)
@@ -27,7 +28,7 @@
     out_ref,
     tok_v, same_v, partner_v, query_v, key_v, value_v, hid_v,
     kv_out, kv_in, kv_mine, kv_all, keys_v, vals_v,
-    qb_out, qb_in, qa_v, q_v, peak_v, acc_v,
+    qb_out, qb_in, qa_v, q_v, peak_v, acc_v, tok_in,
     load_sem, pair_send, pair_recv, ring_send, ring_recv, core_send, core_recv,
 ):
     rows, width, heads, dk, dv = dims
@@ -70,6 +71,14 @@
     for peer in (pair, other, link[Y], link[H], link[M]):
         pl.semaphore_signal(barrier, inc=1, device_id=peer, device_id_type=MESH)
 
+    def to_pair(src, dst, n):
+        return pltpu.make_async_remote_copy(
+            src_ref=src, dst_ref=dst, send_sem=pair_send.at[n], recv_sem=pair_recv.at[n],
+            device_id=pair, device_id_type=MESH,
+        )
+
+    tok_copy = to_pair(tok.at[0, pl.ds(rows - EARLY, EARLY)], tok_in, 2 + chunks)
+
     turned = lax.broadcasted_iota(jnp.int32, (rows, rows), 0) + lax.broadcasted_iota(jnp.int32, (rows, rows), 1)
     turn = jnp.where(turned == rows - 1, 1.0, 0.0).astype(BF16)
 
@@ -92,22 +101,18 @@
             hid_v[:, n * PIECE:(n + 1) * PIECE] = part.astype(BF16)
             if n == 0:
                 begin(q_base, s_base)
+                with jax.named_scope("barrier"):
+                    pl.semaphore_wait(barrier, 5)
+                tok_copy.start()
     begin(s_base, len(loads))
-    def to_pair(src, dst, n):
-        return pltpu.make_async_remote_copy(
-            src_ref=src, dst_ref=dst, send_sem=pair_send.at[n], recv_sem=pair_recv.at[n],
-            device_id=pair, device_id_type=MESH,
-        )
-
     kv_parts = (pl.ds(0, rows), pl.ds(rows, pack - rows))
     kv_copies = [to_pair(kv_out.at[part], kv_in.at[part], n) for n, part in enumerate(kv_parts)]
-    q_copies = [to_pair(qb_out.at[n], qb_in.at[n], 2 + n) for n in range(chunks)]
+    sent = pl.ds(EARLY, rows - EARLY)
+    q_copies = [to_pair(qb_out.at[n, :, sent], qb_in.at[n, :, sent], 2 + n) for n in range(chunks)]
     with jax.named_scope("kB"):
         for n in range(3):
             loads[kv_base + n].wait()
         kv_out[0:rows] = key(hid_v[...]).astype(BF16)
-    with jax.named_scope("barrier"):
-        pl.semaphore_wait(barrier, 5)
     kv_copies[0].start()
     with jax.named_scope("vB"):
         v = value(hid_v[...])
@@ -117,15 +122,14 @@
 
     def heads_of(q):
         for n in range(heads):
-            at = (n % 2) * rows
-            yield n // 2, slice(at, at + rows), q[:, n * dk:(n + 1) * dk]
+            yield n // 2, n % 2, q[:, n * dk:(n + 1) * dk]
 
     with jax.named_scope("qB"):
         loads[q_base].wait()
         q = jnp.dot(hid_v[...], query_v[...], preferred_element_type=F32).astype(BF16)
         q = jnp.dot(turn, q, preferred_element_type=F32).astype(BF16)
-        for n, at, part in heads_of(q):
-            qb_out[n, at] = part
+        for n, h, part in heads_of(q):
+            qb_out[n, h] = part
 
     with jax.named_scope("hA"):
         loads[s_base].wait()
@@ -139,8 +143,8 @@
         kv_mine[2 * rows:] = tail(v)
     with jax.named_scope("qA"):
         q = jnp.dot(hid_v[...], query_v[...], preferred_element_type=F32)
-        for n, at, part in heads_of(q):
-            qa_v[n, at] = part
+        for n, h, part in heads_of(q):
+            qa_v[n, h] = part
 
     with jax.named_scope("w_kv"):
         for copy in kv_copies:
@@ -215,12 +219,12 @@
             with jax.named_scope(f'w_q{c}'):
                 q_copies[c].wait_recv()
         else:
-            for n in range(2, chunks):
+            for n in range(1, chunks - 1):
                 @pl.when(c == n)
                 def _():
                     with jax.named_scope(f"w_q{n}"):
                         q_copies[n].wait_recv()
-        q_v[c] = ((qa_v[c] + qb_in[c].astype(F32)) * scale).astype(BF16)
+        q_v[c] = ((qa_v[c] + qb_in[c].astype(F32)) * scale).astype(BF16).reshape(2 * rows, dk)
 
     def attend(q, places, peak, acc):
         for place in places:
@@ -243,6 +247,16 @@
     q_copies[1].start()
     q_copies[2].start()
 
+    with jax.named_scope("early_q"):
+        tok_copy.wait_recv()
+        for n in range(tiles):
+            part = jnp.dot(tok_in[...], partner_v[n], preferred_element_type=F32)
+            hid_v[0:EARLY, n * PIECE:(n + 1) * PIECE] = part.astype(BF16)
+        q = jnp.dot(hid_v[0:EARLY], query_v[...], preferred_element_type=F32).astype(BF16)
+        q = jnp.dot(turn[rows - EARLY:, 0:EARLY], q, preferred_element_type=F32).astype(BF16)
+        for n, h, part in heads_of(q):
+            qb_in[n, h, 0:EARLY] = part
+
     query(0)
     peak_v[0] = jnp.full(peak_v.shape[1:], -jnp.inf, F32)
     acc_v[0] = jnp.zeros(acc_v.shape[1:], F32)
@@ -267,30 +281,24 @@
             start = jnp.full(peak_v.shape[1:], -jnp.inf, F32), jnp.zeros(acc_v.shape[1:], F32)
             peak_v[c], acc_v[c] = attend(q_v[c], places, *start)
 
-    def second(c, carry):
-        one(c, PLACE[Y ^ H])
+    def early_chunk(c, carry):
+        query(c)
+        begin_chunk(c, range(4))
+
+        @pl.when(c == 1)
+        def _():
+            arrive(Y ^ H)
         return carry
 
-    def late(c, carry):
-        query(c)
-
-        @pl.when(c == chunks - 2)
-        def _():
-            complete(Y ^ H)
-
-        begin_chunk(c, range(5))
-
-        @pl.when(c == chunks - 2)
-        def _():
-            arrive(Y ^ M, H)
-            arrive(M ^ H)
-            lax.fori_loop(0, chunks - 2, second, 0)
-        return carry
-
-    query(1)
-    begin_chunk(1, range(4))
-    arrive(Y ^ H)
-    lax.fori_loop(2, chunks, late, 0)
+    lax.fori_loop(1, chunks - 1, early_chunk, 0)
+    arrive(Y ^ M, H)
+    complete(Y ^ H)
+    with jax.named_scope("ones"):
+        for c in range(chunks - 1):
+            peak_v[c], acc_v[c] = attend(q_v[c], (PLACE[Y ^ H],), peak_v[c], acc_v[c])
+    arrive(M ^ H)
+    query(chunks - 1)
+    begin_chunk(chunks - 1, range(5))
     complete(M ^ H)
     complete(Y ^ M)
     arrive(Y ^ M ^ H)
@@ -318,7 +326,7 @@
     lax.fori_loop(1, chunks, far, 0)
     store(chunks - 1, acc_v[chunks - 1])
 
-    for copy in kv_copies + q_copies:
+    for copy in kv_copies + q_copies + [tok_copy]:
         copy.wait_send()
     for copy in ring.values():
         copy.wait_send()
@@ -352,15 +360,16 @@
             pltpu.VMEM((8, 2, pack, 128), BF16),
             pltpu.VMEM((8, 2 * rows, 128), BF16),
             pltpu.VMEM((8, 2 * rows, 256), BF16),
-            pltpu.VMEM((chunks, 2 * rows, 128), BF16),
-            pltpu.VMEM((chunks, 2 * rows, 128), BF16),
-            pltpu.VMEM((chunks, 2 * rows, 128), F32),
+            pltpu.VMEM((chunks, 2, rows, dk), BF16),
+            pltpu.VMEM((chunks, 2, rows, dk), BF16),
+            pltpu.VMEM((chunks, 2, rows, dk), F32),
             pltpu.VMEM((chunks, 2 * rows, 128), BF16),
             pltpu.VMEM((chunks, 2 * rows, 128), F32),
             pltpu.VMEM((chunks, 2 * rows, 256), F32),
+            pltpu.VMEM((EARLY, width), BF16),
             dma((1 + tiles + 5,)),
-            dma((2 + chunks,)),
-            dma((2 + chunks,)),
+            dma((3 + chunks,)),
+            dma((3 + chunks,)),
             dma((len(SENDS),)),
             dma((len(SENDS),)),
             dma((8,)),

time: 60.1 us -> 58.2 us (0.968)
  Pallas kernels: 57 us -> 55 us
    pallas_call x1, Pallas kernels: 57 us -> 55 us  [body(): pl.pallas_call(functools.partial(kernel, (rows, width, heads, dk, dv)), o...]
where the time goes in v4:
time: 58.2 us; the launch traced here: 58.1 us
  Pallas kernels  55 us (95%)
  matrix products  3 us (5%)
    pallas_call x1, Pallas kernels, body(): pl.pallas_call(functools.partial(kernel, (rows, width, heads, dk, dv)), o...  55 us
    dot_general x1, matrix products, body(): return jnp.dot(mixed, w_out, preferred_element_type=F32).astype(BF16)[None]  3 us

profile of v4, /device:TPU:1, one launch (start us, length us, event | category | flops | bytes accessed | tf_op | source)
XLA Modules:
  0.0 58.1 jit_solution(6847100683815230777)
XLA Ops:
  0.0 0.0 copy-start
  0.0 55.0 %strand_attention.1 = bf16[384,1536]{1,0:T(8,128)(2,1)S(1)} custom-call(bf16[1,384,1536]{2,1,0:T(8,128)(2,1)} %tok.1, bf16[1536,1536]{1,0:T(8,128)(2,1)} %w_same.1, bf16[1536,1536]{1,0:T(8,128)(2,1)} %w_partner.1, bf16[1536,1024]{1,0:T(8,128)(2,1)} %w_query.1, bf16[1536,128]{1,0:T(8,128)(2,1)} %w_key.1, bf16[192,1536]{1,0:T(8,128)(2,1)} %bitcast.5), custom_call_target="tpu_custom_call" | custom-call | tf_op jit(solution)/shard_map/strand_attention/pallas_call | solution.py:344
  55.1 0.0 copy-done
  55.1 3.0 %fusion = bf16[1,384,1536]{2,1,0:T(8,128)(2,1)} fusion(bf16[384,1536]{1,0:T(8,128)(2,1)S(1)} %strand_attention.1, bf16[1536,1536]{1,0:T(8,128)(2,1)S(1)} %copy-done), kind=kOutput, calls=%fused_computation.1 | convolution fusion | flops 1812529152 | bytes 7077888 | tf_op jit(solution)/shard_map/dot_general | solution.py:383
Async XLA Ops:
  0.0 55.1 %copy-start = (bf16[1536,1536]{1,0:T(8,128)(2,1)S(1)}, bf16[1536,1536]{1,0:T(8,128)(2,1)}, u32[]{:S(2)}) copy-start(bf16[1536,1536]{1,0:T(8,128)(2,1)} %param.13) | copy-start | bytes 14155780

commit v5 on v4

--- a/solution.py
+++ b/solution.py
@@ -99,8 +99,9 @@
             loads[1 + n].wait()
             part = jnp.dot(tok_v[...], partner_v[n], preferred_element_type=F32)
             hid_v[:, n * PIECE:(n + 1) * PIECE] = part.astype(BF16)
+            if n == 1:
+                begin(q_base, s_base)
             if n == 0:
-                begin(q_base, s_base)
                 with jax.named_scope("barrier"):
                     pl.semaphore_wait(barrier, 5)
                 tok_copy.start()
@@ -303,9 +304,12 @@
     complete(Y ^ M)
     arrive(Y ^ M ^ H)
     with jax.named_scope("two"):
-        peak_v[0], acc_v[0] = attend(q_v[0], (5, 6), peak_v[0], acc_v[0])
+        for c in range(2):
+            peak_v[c], acc_v[c] = attend(q_v[c], (5, 6), peak_v[c], acc_v[c])
     complete(Y ^ M ^ H)
-    one(0, 7)
+    with jax.named_scope("one"):
+        for c in range(2):
+            _, acc_v[c] = attend(q_v[c], (7,), peak_v[c], acc_v[c])
 
     def store(c, acc):
         mixed = acc * (1.0 / acc[:, dv:dv + 1])
@@ -323,7 +327,8 @@
             _, acc_v[c] = attend(q_v[c], range(5, 8), peak_v[c], acc_v[c])
         return carry
 
-    lax.fori_loop(1, chunks, far, 0)
+    store(0, acc_v[0])
+    lax.fori_loop(2, chunks, far, 0)
     store(chunks - 1, acc_v[chunks - 1])
 
     for copy in kv_copies + q_copies + [tok_copy]:

time: 58.2 us -> 58 us (level)
  no operation moved by 1% of the time
where the time goes in v5:
time: 58 us; the launch traced here: 57.9 us
  Pallas kernels  54.9 us (95%)
  matrix products  3 us (5%)
    pallas_call x1, Pallas kernels, body(): pl.pallas_call(functools.partial(kernel, (rows, width, heads, dk, dv)), o...  54.9 us
    dot_general x1, matrix products, body(): return jnp.dot(mixed, w_out, preferred_element_type=F32).astype(BF16)[None]  3 us

profile of v5, /device:TPU:1, one launch (start us, length us, event | category | flops | bytes accessed | tf_op | source)
XLA Modules:
  0.0 57.9 jit_solution(9859264908278717533)
XLA Ops:
  0.0 0.0 copy-start
  0.0 54.9 %strand_attention.1 = bf16[384,1536]{1,0:T(8,128)(2,1)S(1)} custom-call(bf16[1,384,1536]{2,1,0:T(8,128)(2,1)} %tok.1, bf16[1536,1536]{1,0:T(8,128)(2,1)} %w_same.1, bf16[1536,1536]{1,0:T(8,128)(2,1)} %w_partner.1, bf16[1536,1024]{1,0:T(8,128)(2,1)} %w_query.1, bf16[1536,128]{1,0:T(8,128)(2,1)} %w_key.1, bf16[192,1536]{1,0:T(8,128)(2,1)} %bitcast.5), custom_call_target="tpu_custom_call" | custom-call | tf_op jit(solution)/shard_map/strand_attention/pallas_call | solution.py:349
  54.9 0.0 copy-done
  54.9 3.0 %fusion = bf16[1,384,1536]{2,1,0:T(8,128)(2,1)} fusion(bf16[384,1536]{1,0:T(8,128)(2,1)S(1)} %strand_attention.1, bf16[1536,1536]{1,0:T(8,128)(2,1)S(1)} %copy-done), kind=kOutput, calls=%fused_computation.1 | convolution fusion | flops 1812529152 | bytes 7077888 | tf_op jit(solution)/shard_map/dot_general | solution.py:388
Async XLA Ops:
  0.0 54.9 %copy-start = (bf16[1536,1536]{1,0:T(8,128)(2,1)S(1)}, bf16[1536,1536]{1,0:T(8,128)(2,1)}, u32[]{:S(2)}) copy-start(bf16[1536,1536]{1,0:T(8,128)(2,1)} %param.13) | copy-start | bytes 14155780
